TPU v7x, 256 devices: a whole 4x4x8 slice. The times are simulated.
256 devices in a mesh: tm: 16 (over y_lo, x, core), blk: 8 (over z), samp: 2 (over y_hi).
Axes of the slice: x: 4, y: 4 (y_hi: 2, y_lo: 2; y = y_hi * 2 + y_lo), z: 8, core: 2. Of those that a mesh axis runs over, the one named last changes fastest.
Arguments:
- prior_path: float32 [32, 16, 1024], P('tm', 'samp', 'blk'), may hold values from -6 to 6
- observed: float32 [32, 256], P('tm', 'blk'), may hold values from -6 to 6
- obs_mask: int32 [32, 32], P('tm', 'blk'), may hold values 0 or 1
- noise_draw: float32 [32, 16, 256], P('tm', 'samp', 'blk'), may hold values from -6 to 6
- wend_blocks: float32 [128, 8, 8], P('blk'), may hold values from -1 to 1
- block_cols: int32 [128], P('blk'), may hold values from 0 to 31, as said below
- start_mean: float32 [16, 1024], P('samp', 'blk'), may hold values from -6 to 6
- trans_mats: bfloat16 [32, 1024, 1024], P('tm', 'blk', 'samp')
- gain_mats: bfloat16 [32, 1024, 256], P('tm', 'blk', 'samp'), may hold values from -0.375 to 0.375
- smooth_mats: bfloat16 [32, 1024, 1024], P('tm', 'blk', 'samp')
- site_trans: float32 [4, 4], replicated, may hold values from -2.5 to 2.5
Outputs:
- posterior_path: float32 [32, 16, 1024], P('tm', 'samp', 'blk')
Inputs may be any that keep to these rules, and one draw needn't show every extreme that they name: `block_cols`: entry 4 i names block i itself, entries 4 i + 1 to 4 i + 3 name three different blocks among i - 2, i - 1, i + 1, i + 2 taken modulo 32.
All inputs are finite; a program needn't handle non-finite values. No bound on the sum of `obs_mask` on one device may be relied on, other than what follows from the above.
Results may differ from a plain program's by a relative error of at most 0.0003.
Values may be sent and summed in bfloat16 or wider, within the bound.
No kernel may reach another device: no remote copies, remote signals or barrier semaphores. Data moves between devices by JAX's collectives and lax.ppermute only.
A program may use at most 64 MiB of HBM per device.

v0:
```python
import jax
import jax.numpy as jnp
from jax import lax
from jax.sharding import PartitionSpec as P

highest = lax.Precision.HIGHEST


def with_halo(value, sides, width):
    for axis, dim in sides:
        count, length = (lax.axis_size(axis), value.shape[dim])
        up = [(i, (i + 1) % count) for i in range(count)]
        down = [(j, i) for i, j in up]
        last = lax.slice_in_dim(value, length - width, length, axis=dim)
        initial = lax.slice_in_dim(value, 0, width, axis=dim)
        before = lax.ppermute(last, axis, up)
        after = lax.ppermute(initial, axis, down)
        value = jnp.concatenate([before, value, after], axis=dim)
    return value


def shifted(value, axis, steps):
    count = lax.axis_size(axis)
    initial, last = (max(0, -steps), min(count, count - steps))
    return lax.ppermute(value, axis, [(source, source + steps) for source in range(initial, last)])


def apply_rows(matrix, states):
    return jnp.einsum("ij,sj->si", matrix, states, precision=highest)


def on_device(
    prior_path,
    observed,
    obs_mask,
    noise_draw,
    wend_blocks,
    block_cols,
    start_mean,
    trans_mats,
    gain_mats,
    smooth_mats,
    site_trans,
):
    trans_mats, gain_mats, smooth_mats = (
        lax.all_gather(trans_mats, "samp", axis=2, tiled=True),
        lax.all_gather(gain_mats, "samp", axis=2, tiled=True),
        lax.all_gather(smooth_mats, "samp", axis=2, tiled=True),
    )
    step_count, sample_count, local_sites = noise_draw.shape
    block_sites = wend_blocks.shape[1]
    local_blocks = local_sites // block_sites
    cycle_size = lax.axis_size("blk")
    block_count = local_blocks * cycle_size
    row_count = trans_mats.shape[1]
    state_count = row_count * cycle_size
    widened = with_halo(noise_draw, (("blk", 2),), 2 * block_sites)
    rim_blocks = widened.reshape(step_count, sample_count, local_blocks + 4, block_sites)
    pair_rows = jnp.arange(local_blocks * 4, dtype=jnp.int32) // 4
    first_block = lax.axis_index("blk") * local_blocks
    offset = (block_cols - first_block - pair_rows + 2) % block_count
    position = pair_rows + offset
    chooser = (position[:, None] == jnp.arange(local_blocks + 4, dtype=jnp.int32)[None, :]).astype(
        jnp.float32
    )
    picked = jnp.einsum("pl,tslj->tspj", chooser, rim_blocks, precision=highest)
    mixed = jnp.einsum("tspj,pij->tspi", picked, wend_blocks, precision=highest)
    obs_noise = jnp.sum(
        mixed.reshape(step_count, sample_count, local_blocks, 4, block_sites), axis=3
    ).reshape(step_count, sample_count, local_sites)
    first_comp = prior_path.reshape(step_count, sample_count, local_sites, 4)[:, :, :, 0]
    seen_mask = jnp.repeat(obs_mask.astype(jnp.float32), block_sites, axis=1)
    residual = seen_mask[:, None, :] * (observed[:, None, :] - first_comp - obs_noise)
    all_resid = lax.all_gather(residual, "blk", axis=2, tiled=True)
    inputs = jnp.einsum("tij,tsj->tsi", gain_mats, all_resid, precision=highest)
    left_trans = trans_mats[1]
    left_smooth = smooth_mats[0]
    forward_pair = jnp.dot(
        left_trans,
        lax.all_gather(trans_mats[0], "blk", axis=0, tiled=True),
        preferred_element_type=jnp.float32,
    )
    backward_pair = jnp.dot(
        left_smooth,
        lax.all_gather(smooth_mats[1], "blk", axis=0, tiled=True),
        preferred_element_type=jnp.float32,
    )
    first_input, initial = (
        lax.all_gather(inputs[0], "blk", axis=1, tiled=True),
        lax.all_gather(start_mean, "blk", axis=1, tiled=True),
    )
    carry_input = apply_rows(trans_mats[1], first_input) + inputs[1]
    is_first = lax.axis_index("tm") == 0
    time_size = lax.axis_size("tm")
    level_count = (time_size - 1).bit_length()
    matrix, vector = shifted((forward_pair, carry_input), "tm", 1)
    vector = jnp.where(is_first, start_mean, vector)
    for level in range(level_count):
        received_m, received_v = shifted((matrix, vector), "tm", 1 << level)
        complete_m, complete_v = (
            lax.all_gather(received_m, "blk", axis=0, tiled=True),
            lax.all_gather(received_v, "blk", axis=1, tiled=True),
        )
        matrix, vector = (
            jnp.dot(matrix, complete_m, precision=highest),
            apply_rows(matrix, complete_v) + vector,
        )
    entry_state = lax.all_gather(vector, "blk", axis=1, tiled=True)
    filtered = jnp.stack(
        [
            apply_rows(trans_mats[0], entry_state) + inputs[0],
            apply_rows(forward_pair, entry_state) + carry_input,
        ]
    )
    site_kron = jnp.kron(jnp.eye(row_count // 4, dtype=jnp.float32), site_trans)
    predicted = jnp.einsum("ij,tsj->tsi", site_kron, filtered, precision=highest)
    all_pred = lax.all_gather(predicted, "blk", axis=2, tiled=True)
    offsets = filtered - jnp.einsum("tij,tsj->tsi", smooth_mats, all_pred, precision=highest)
    is_last = lax.axis_index("tm") == time_size - 1
    late_offset = jnp.where(is_last, filtered[1], offsets[1])
    all_late = lax.all_gather(late_offset, "blk", axis=1, tiled=True)
    back_offset = apply_rows(smooth_mats[0], all_late) + offsets[0]

    def relay_back(relay_turn, later_now):
        emitted = apply_rows(backward_pair, later_now) + back_offset
        complete = lax.all_gather(emitted, "blk", axis=1, tiled=True)
        received = shifted(complete, "tm", -1)
        return jnp.where(lax.axis_index("tm") == time_size - 2 - relay_turn, received, later_now)

    later_state = lax.fori_loop(
        0, time_size - 1, relay_back, jnp.zeros((sample_count, state_count), jnp.float32)
    )
    smoothed = jnp.stack(
        [
            apply_rows(backward_pair, later_state) + back_offset,
            apply_rows(smooth_mats[1], later_state) + late_offset,
        ]
    )
    return prior_path + smoothed


def solution(mesh):
    placed = (
        P("tm", "samp", "blk"),
        P("tm", "blk"),
        P("tm", "blk"),
        P("tm", "samp", "blk"),
        P("blk", None, None),
        P("blk"),
        P("samp", "blk"),
        P("tm", "blk", "samp"),
        P("tm", "blk", "samp"),
        P("tm", "blk", "samp"),
        P(),
    )
    return jax.shard_map(
        on_device, mesh=mesh, in_specs=placed, out_specs=P("tm", "samp", "blk"), check_vma=False
    )
```

profile of v0, /device:TPU:7, one launch (start us, length us, event | category | flops | bytes accessed | tf_op | source)
XLA Modules:
  0.0 952.8 jit_solution(16144380244082695753)
XLA Ops:
  16.9 41.3 %all-gather.17.cloned.1.call-done = bf16[1,1024,1024]{2,1,0:T(8,128)(2,1)} async-done(((bf16[1,128,1024]{2,1,0:T(8,128)(2,1)}), bf16[1,1024,1024]{2,1,0:T(8,128)(2,1)}) %all-gather.17.cloned.1.call-update) | async-done | bytes 2097168 | tf_op jit(solution)/shard_map/all_gather | solution.py:80
  87.2 53.6 %all-gather.9.cloned.1.call-done = f32[1024,1024]{1,0:T(8,128)} async-done(((f32[128,1024]{1,0:T(8,128)}), f32[1024,1024]{1,0:T(8,128)}) %all-gather.9.cloned.1.call-update) | async-done | bytes 4194320 | tf_op jit(solution)/shard_map/all_gather | solution.py:101
  170.5 45.1 %all-gather.11.cloned.1.call-done = f32[1024,1024]{1,0:T(8,128)} async-done(((f32[128,1024]{1,0:T(8,128)}), f32[1024,1024]{1,0:T(8,128)}) %all-gather.11.cloned.1.call-update) | async-done | bytes 4194320 | tf_op jit(solution)/shard_map/all_gather | solution.py:101
  246.9 19.8 %all_gather.60 = f32[2,8,256]{1,0,2:T(2,128)S(1)} all-gather(f32[2,8,32]{1,0,2:T(2,128)S(1)} %copy.27), channel_id=1, replica_groups=mesh['tm'=16,'blk'=8,'samp'=2] {'blk'}, dimensions={2}, use_global_device_ids=true | all-gather | bytes 18432 | tf_op jit(solution)/shard_map/all_gather | solution.py:74
  267.0 20.3 %all-gather.1 = f32[1,8,1024]{2,1,0:T(8,128)S(1)} all-gather(f32[1,8,128]{2,1,0:T(8,128)S(1)} %slice.52), channel_id=3, replica_groups=mesh['tm'=16,'blk'=8,'samp'=2] {'blk'}, dimensions={2}, use_global_device_ids=true | all-gather | bytes 36864 | tf_op jit(solution)/shard_map/all_gather | solution.py:89
  359.5 18.3 %all_gather.68 = f32[8,1024]{1,0:T(8,128)S(1)} all-gather(f32[8,128]{1,0:T(8,128)S(1)} %collective-permute-done.8), channel_id=1, replica_groups=mesh['tm'=16,'blk'=8,'samp'=2] {'blk'}, dimensions={1}, use_global_device_ids=true | all-gather | bytes 36864 | tf_op jit(solution)/shard_map/all_gather | solution.py:102
  405.0 18.2 %all_gather.72 = f32[8,1024]{1,0:T(8,128)S(1)} all-gather(f32[8,128]{1,0:T(8,128)S(1)} %convolution_add_fusion.7), channel_id=1, replica_groups=mesh['tm'=16,'blk'=8,'samp'=2] {'blk'}, dimensions={1}, use_global_device_ids=true | all-gather | bytes 36864 | tf_op jit(solution)/shard_map/all_gather | solution.py:108
  424.2 18.2 %all_gather.73 = f32[2,8,1024]{2,1,0:T(8,128)S(1)} all-gather(f32[2,8,128]{2,1,0:T(8,128)S(1)} %fusion.18), channel_id=1, replica_groups=mesh['tm'=16,'blk'=8,'samp'=2] {'blk'}, dimensions={2}, use_global_device_ids=true | all-gather | bytes 73728 | tf_op jit(solution)/shard_map/all_gather | solution.py:117
  461.3 483.5 %while.14 = (s32[]{:T(128)}, f32[8,1024]{1,0:T(8,128)S(1)}, f32[128,1024]{1,0:T(8,128)S(1)}, f32[8,128]{1,0:T(8,128)S(1)}, s32[]{:T(128)}, /*index=5*/s32[]{:T(128)}, u32[]{:T(128)}, u32[]{:T(128)}, s32[]{:T(128)}) while((s32[]{:T(128)}, f32[8,1024]{1,0:T(8,128)S(1)}, f32[128,1024]{1,0:T(8,128)S(1)}, f32[8,128]{1,0:T(8,128)S(1)}, ...), condition=%wide.region_2.3_spmd.clone, body=%wide.region_1.2_spmd.clone.sunk | while | flops 12608520 | bytes 831686 | solution.py:130
  461.8 18.2 %all_gather.77 = f32[8,1024]{1,0:T(8,128)S(1)} all-gather(f32[8,128]{1,0:T(8,128)S(1)} %convolution_add_fusion.12), channel_id=1, replica_groups=mesh['tm'=16,'blk'=8,'samp'=2] {'blk'}, dimensions={1}, use_global_device_ids=true | all-gather | bytes 36864 | tf_op jit(solution)/shard_map/while/body/eval_jaxpr/all_gather | solution.py:126
  480.0 57.5 %collective-permute-start = (f32[8,1024]{1,0:T(8,128)S(1)}, f32[8,1024]{1,0:T(8,128)S(1)}, u32[]{:S(2)}, u32[]{:S(2)}) collective-permute-start(f32[8,1024]{1,0:T(8,128)S(1)} %all_gather.77), channel_id=1, source_target_pairs={{16,0},{32,16},{48,32},{64,48},{80,64},{96,80},{112,96},{128,112},... | collective-permute-start | bytes 98312 | tf_op jit(solution)/shard_map/while/body/eval_jaxpr/ppermute | solution.py:25
  546.5 18.2 %all_gather.77 = f32[8,1024]{1,0:T(8,128)S(1)} all-gather(f32[8,128]{1,0:T(8,128)S(1)} %convolution_add_fusion.12), channel_id=1, replica_groups=mesh['tm'=16,'blk'=8,'samp'=2] {'blk'}, dimensions={1}, use_global_device_ids=true | all-gather | bytes 36864 | tf_op jit(solution)/shard_map/while/body/eval_jaxpr/all_gather | solution.py:126
  575.0 18.2 %all_gather.77 = f32[8,1024]{1,0:T(8,128)S(1)} all-gather(f32[8,128]{1,0:T(8,128)S(1)} %convolution_add_fusion.12), channel_id=1, replica_groups=mesh['tm'=16,'blk'=8,'samp'=2] {'blk'}, dimensions={1}, use_global_device_ids=true | all-gather | bytes 36864 | tf_op jit(solution)/shard_map/while/body/eval_jaxpr/all_gather | solution.py:126
  603.4 18.2 %all_gather.77 = f32[8,1024]{1,0:T(8,128)S(1)} all-gather(f32[8,128]{1,0:T(8,128)S(1)} %convolution_add_fusion.12), channel_id=1, replica_groups=mesh['tm'=16,'blk'=8,'samp'=2] {'blk'}, dimensions={1}, use_global_device_ids=true | all-gather | bytes 36864 | tf_op jit(solution)/shard_map/while/body/eval_jaxpr/all_gather | solution.py:126
  631.9 18.2 %all_gather.77 = f32[8,1024]{1,0:T(8,128)S(1)} all-gather(f32[8,128]{1,0:T(8,128)S(1)} %convolution_add_fusion.12), channel_id=1, replica_groups=mesh['tm'=16,'blk'=8,'samp'=2] {'blk'}, dimensions={1}, use_global_device_ids=true | all-gather | bytes 36864 | tf_op jit(solution)/shard_map/while/body/eval_jaxpr/all_gather | solution.py:126
  660.4 18.2 %all_gather.77 = f32[8,1024]{1,0:T(8,128)S(1)} all-gather(f32[8,128]{1,0:T(8,128)S(1)} %convolution_add_fusion.12), channel_id=1, replica_groups=mesh['tm'=16,'blk'=8,'samp'=2] {'blk'}, dimensions={1}, use_global_device_ids=true | all-gather | bytes 36864 | tf_op jit(solution)/shard_map/while/body/eval_jaxpr/all_gather | solution.py:126
  717.4 18.2 %all_gather.77 = f32[8,1024]{1,0:T(8,128)S(1)} all-gather(f32[8,128]{1,0:T(8,128)S(1)} %convolution_add_fusion.12), channel_id=1, replica_groups=mesh['tm'=16,'blk'=8,'samp'=2] {'blk'}, dimensions={1}, use_global_device_ids=true | all-gather | bytes 36864 | tf_op jit(solution)/shard_map/while/body/eval_jaxpr/all_gather | solution.py:126
  745.9 18.2 %all_gather.77 = f32[8,1024]{1,0:T(8,128)S(1)} all-gather(f32[8,128]{1,0:T(8,128)S(1)} %convolution_add_fusion.12), channel_id=1, replica_groups=mesh['tm'=16,'blk'=8,'samp'=2] {'blk'}, dimensions={1}, use_global_device_ids=true | all-gather | bytes 36864 | tf_op jit(solution)/shard_map/while/body/eval_jaxpr/all_gather | solution.py:126
  774.3 18.2 %all_gather.77 = f32[8,1024]{1,0:T(8,128)S(1)} all-gather(f32[8,128]{1,0:T(8,128)S(1)} %convolution_add_fusion.12), channel_id=1, replica_groups=mesh['tm'=16,'blk'=8,'samp'=2] {'blk'}, dimensions={1}, use_global_device_ids=true | all-gather | bytes 36864 | tf_op jit(solution)/shard_map/while/body/eval_jaxpr/all_gather | solution.py:126
  802.8 18.2 %all_gather.77 = f32[8,1024]{1,0:T(8,128)S(1)} all-gather(f32[8,128]{1,0:T(8,128)S(1)} %convolution_add_fusion.12), channel_id=1, replica_groups=mesh['tm'=16,'blk'=8,'samp'=2] {'blk'}, dimensions={1}, use_global_device_ids=true | all-gather | bytes 36864 | tf_op jit(solution)/shard_map/while/body/eval_jaxpr/all_gather | solution.py:126
  831.3 18.2 %all_gather.77 = f32[8,1024]{1,0:T(8,128)S(1)} all-gather(f32[8,128]{1,0:T(8,128)S(1)} %convolution_add_fusion.12), channel_id=1, replica_groups=mesh['tm'=16,'blk'=8,'samp'=2] {'blk'}, dimensions={1}, use_global_device_ids=true | all-gather | bytes 36864 | tf_op jit(solution)/shard_map/while/body/eval_jaxpr/all_gather | solution.py:126
  859.8 18.2 %all_gather.77 = f32[8,1024]{1,0:T(8,128)S(1)} all-gather(f32[8,128]{1,0:T(8,128)S(1)} %convolution_add_fusion.12), channel_id=1, replica_groups=mesh['tm'=16,'blk'=8,'samp'=2] {'blk'}, dimensions={1}, use_global_device_ids=true | all-gather | bytes 36864 | tf_op jit(solution)/shard_map/while/body/eval_jaxpr/all_gather | solution.py:126
  888.3 18.2 %all_gather.77 = f32[8,1024]{1,0:T(8,128)S(1)} all-gather(f32[8,128]{1,0:T(8,128)S(1)} %convolution_add_fusion.12), channel_id=1, replica_groups=mesh['tm'=16,'blk'=8,'samp'=2] {'blk'}, dimensions={1}, use_global_device_ids=true | all-gather | bytes 36864 | tf_op jit(solution)/shard_map/while/body/eval_jaxpr/all_gather | solution.py:126
  916.8 18.2 %all_gather.77 = f32[8,1024]{1,0:T(8,128)S(1)} all-gather(f32[8,128]{1,0:T(8,128)S(1)} %convolution_add_fusion.12), channel_id=1, replica_groups=mesh['tm'=16,'blk'=8,'samp'=2] {'blk'}, dimensions={1}, use_global_device_ids=true | all-gather | bytes 36864 | tf_op jit(solution)/shard_map/while/body/eval_jaxpr/all_gather | solution.py:126
  (179 shorter events, 392.2 us)
Async XLA Ops:
  6.5 51.7 %all-gather.17.cloned.1.call-start = ((), (), s32[]{:S(2)}) async-start(), calls=%async_computation.4 | async-start | bytes 2359296 | tf_op jit(solution)/shard_map/all_gather | solution.py:80
  16.9 123.9 %all-gather.9.cloned.1.call-start = ((), (), s32[]{:S(2)}) async-start(), calls=%async_computation | async-start | bytes 4718592 | tf_op jit(solution)/shard_map/all_gather | solution.py:101
  60.3 13.5 %collective-permute-start.5 = (f32[128,1024]{1,0:T(8,128)S(1)}, f32[128,1024]{1,0:T(8,128)S(1)}, u32[]{:S(2)}, u32[]{:S(2)}) collective-permute-start(f32[128,1024]{1,0:T(8,128)S(1)} %fusion.4), channel_id=1, source_target_pairs={{0,16},{16,32},{32,48},{48,64},{64,80},{80,96},{96,112},{112,128},... | collective-permute-start | bytes 1572872 | tf_op jit(solution)/shard_map/ppermute | solution.py:25
  73.7 12.6 %collective-permute-start.7 = (f32[128,1024]{1,0:T(8,128)S(1)}, f32[128,1024]{1,0:T(8,128)S(1)}, u32[]{:S(2)}, u32[]{:S(2)}) collective-permute-start(f32[128,1024]{1,0:T(8,128)S(1)} %collective-permute-done.5), channel_id=1, source_target_pairs={{0,16},{16,32},{32,48},{48,64},{64,80},{80,96},{96,112},{112,128},... | collective-permute-start | bytes 1572872 | tf_op jit(solution)/shard_map/ppermute | solution.py:25
  87.2 128.5 %all-gather.11.cloned.1.call-start = ((), (), s32[]{:S(2)}) async-start(), calls=%async_computation.1 | async-start | bytes 4718592 | tf_op jit(solution)/shard_map/all_gather | solution.py:101
  145.5 14.8 %collective-permute-start.9 = (f32[128,1024]{1,0:T(8,128)S(1)}, f32[128,1024]{1,0:T(8,128)S(1)}, u32[]{:S(2)}, u32[]{:S(2)}) collective-permute-start(f32[128,1024]{1,0:T(8,128)S(1)} %fusion.29), channel_id=1, source_target_pairs={{0,32},{16,48},{32,64},{48,80},{64,96},{80,112},{96,128},{112,144}... | collective-permute-start | bytes 1572872 | tf_op jit(solution)/shard_map/ppermute | solution.py:25
  161.2 218.6 %all-gather.15.cloned.1.call-start = ((), (), s32[]{:S(2)}) async-start(), calls=%async_computation.3 | async-start | bytes 2359296 | tf_op jit(solution)/shard_map/all_gather | solution.py:85
  170.5 229.5 %all-gather.13.cloned.1.call-start = ((), (), s32[]{:S(2)}) async-start(), calls=%async_computation.2 | async-start | bytes 4718592 | tf_op jit(solution)/shard_map/all_gather | solution.py:101
  220.2 16.2 %collective-permute-start.11 = (f32[128,1024]{1,0:T(8,128)S(1)}, f32[128,1024]{1,0:T(8,128)S(1)}, u32[]{:S(2)}, u32[]{:S(2)}) collective-permute-start(f32[128,1024]{1,0:T(8,128)S(1)} %fusion.30), channel_id=1, source_target_pairs={{0,64},{16,80},{32,96},{48,112},{64,128},{80,144},{96,160},{112,17... | collective-permute-start | bytes 1572872 | tf_op jit(solution)/shard_map/ppermute | solution.py:25
  287.5 17.6 %collective-permute-start.3 = (f32[8,128]{1,0:T(8,128)S(1)}, f32[8,128]{1,0:T(8,128)S(1)}, u32[]{:S(2)}, u32[]{:S(2)}) collective-permute-start(f32[8,128]{1,0:T(8,128)S(1)} %convolution_add_fusion.4), channel_id=1, source_target_pairs={{0,16},{16,32},{32,48},{48,64},{64,80},{80,96},{96,112},{112,128},... | collective-permute-start | bytes 12296 | tf_op jit(solution)/shard_map/ppermute | solution.py:25
  480.0 66.1 %collective-permute-start = (f32[8,1024]{1,0:T(8,128)S(1)}, f32[8,1024]{1,0:T(8,128)S(1)}, u32[]{:S(2)}, u32[]{:S(2)}) collective-permute-start(f32[8,1024]{1,0:T(8,128)S(1)} %all_gather.77), channel_id=1, source_target_pairs={{16,0},{32,16},{48,32},{64,48},{80,64},{96,80},{112,96},{128,112},... | collective-permute-start | bytes 98312 | tf_op jit(solution)/shard_map/while/body/eval_jaxpr/ppermute | solution.py:25
  564.7 9.9 %collective-permute-start = (f32[8,1024]{1,0:T(8,128)S(1)}, f32[8,1024]{1,0:T(8,128)S(1)}, u32[]{:S(2)}, u32[]{:S(2)}) collective-permute-start(f32[8,1024]{1,0:T(8,128)S(1)} %all_gather.77), channel_id=1, source_target_pairs={{16,0},{32,16},{48,32},{64,48},{80,64},{96,80},{112,96},{128,112},... | collective-permute-start | bytes 98312 | tf_op jit(solution)/shard_map/while/body/eval_jaxpr/ppermute | solution.py:25
  593.1 9.9 %collective-permute-start = (f32[8,1024]{1,0:T(8,128)S(1)}, f32[8,1024]{1,0:T(8,128)S(1)}, u32[]{:S(2)}, u32[]{:S(2)}) collective-permute-start(f32[8,1024]{1,0:T(8,128)S(1)} %all_gather.77), channel_id=1, source_target_pairs={{16,0},{32,16},{48,32},{64,48},{80,64},{96,80},{112,96},{128,112},... | collective-permute-start | bytes 98312 | tf_op jit(solution)/shard_map/while/body/eval_jaxpr/ppermute | solution.py:25
  621.6 9.9 %collective-permute-start = (f32[8,1024]{1,0:T(8,128)S(1)}, f32[8,1024]{1,0:T(8,128)S(1)}, u32[]{:S(2)}, u32[]{:S(2)}) collective-permute-start(f32[8,1024]{1,0:T(8,128)S(1)} %all_gather.77), channel_id=1, source_target_pairs={{16,0},{32,16},{48,32},{64,48},{80,64},{96,80},{112,96},{128,112},... | collective-permute-start | bytes 98312 | tf_op jit(solution)/shard_map/while/body/eval_jaxpr/ppermute | solution.py:25
  650.1 9.9 %collective-permute-start = (f32[8,1024]{1,0:T(8,128)S(1)}, f32[8,1024]{1,0:T(8,128)S(1)}, u32[]{:S(2)}, u32[]{:S(2)}) collective-permute-start(f32[8,1024]{1,0:T(8,128)S(1)} %all_gather.77), channel_id=1, source_target_pairs={{16,0},{32,16},{48,32},{64,48},{80,64},{96,80},{112,96},{128,112},... | collective-permute-start | bytes 98312 | tf_op jit(solution)/shard_map/while/body/eval_jaxpr/ppermute | solution.py:25
  678.6 9.9 %collective-permute-start = (f32[8,1024]{1,0:T(8,128)S(1)}, f32[8,1024]{1,0:T(8,128)S(1)}, u32[]{:S(2)}, u32[]{:S(2)}) collective-permute-start(f32[8,1024]{1,0:T(8,128)S(1)} %all_gather.77), channel_id=1, source_target_pairs={{16,0},{32,16},{48,32},{64,48},{80,64},{96,80},{112,96},{128,112},... | collective-permute-start | bytes 98312 | tf_op jit(solution)/shard_map/while/body/eval_jaxpr/ppermute | solution.py:25
  707.1 9.9 %collective-permute-start = (f32[8,1024]{1,0:T(8,128)S(1)}, f32[8,1024]{1,0:T(8,128)S(1)}, u32[]{:S(2)}, u32[]{:S(2)}) collective-permute-start(f32[8,1024]{1,0:T(8,128)S(1)} %all_gather.77), channel_id=1, source_target_pairs={{16,0},{32,16},{48,32},{64,48},{80,64},{96,80},{112,96},{128,112},... | collective-permute-start | bytes 98312 | tf_op jit(solution)/shard_map/while/body/eval_jaxpr/ppermute | solution.py:25
  735.6 9.9 %collective-permute-start = (f32[8,1024]{1,0:T(8,128)S(1)}, f32[8,1024]{1,0:T(8,128)S(1)}, u32[]{:S(2)}, u32[]{:S(2)}) collective-permute-start(f32[8,1024]{1,0:T(8,128)S(1)} %all_gather.77), channel_id=1, source_target_pairs={{16,0},{32,16},{48,32},{64,48},{80,64},{96,80},{112,96},{128,112},... | collective-permute-start | bytes 98312 | tf_op jit(solution)/shard_map/while/body/eval_jaxpr/ppermute | solution.py:25
  764.0 9.9 %collective-permute-start = (f32[8,1024]{1,0:T(8,128)S(1)}, f32[8,1024]{1,0:T(8,128)S(1)}, u32[]{:S(2)}, u32[]{:S(2)}) collective-permute-start(f32[8,1024]{1,0:T(8,128)S(1)} %all_gather.77), channel_id=1, source_target_pairs={{16,0},{32,16},{48,32},{64,48},{80,64},{96,80},{112,96},{128,112},... | collective-permute-start | bytes 98312 | tf_op jit(solution)/shard_map/while/body/eval_jaxpr/ppermute | solution.py:25
  792.5 9.9 %collective-permute-start = (f32[8,1024]{1,0:T(8,128)S(1)}, f32[8,1024]{1,0:T(8,128)S(1)}, u32[]{:S(2)}, u32[]{:S(2)}) collective-permute-start(f32[8,1024]{1,0:T(8,128)S(1)} %all_gather.77), channel_id=1, source_target_pairs={{16,0},{32,16},{48,32},{64,48},{80,64},{96,80},{112,96},{128,112},... | collective-permute-start | bytes 98312 | tf_op jit(solution)/shard_map/while/body/eval_jaxpr/ppermute | solution.py:25
  821.0 9.9 %collective-permute-start = (f32[8,1024]{1,0:T(8,128)S(1)}, f32[8,1024]{1,0:T(8,128)S(1)}, u32[]{:S(2)}, u32[]{:S(2)}) collective-permute-start(f32[8,1024]{1,0:T(8,128)S(1)} %all_gather.77), channel_id=1, source_target_pairs={{16,0},{32,16},{48,32},{64,48},{80,64},{96,80},{112,96},{128,112},... | collective-permute-start | bytes 98312 | tf_op jit(solution)/shard_map/while/body/eval_jaxpr/ppermute | solution.py:25
  849.5 9.9 %collective-permute-start = (f32[8,1024]{1,0:T(8,128)S(1)}, f32[8,1024]{1,0:T(8,128)S(1)}, u32[]{:S(2)}, u32[]{:S(2)}) collective-permute-start(f32[8,1024]{1,0:T(8,128)S(1)} %all_gather.77), channel_id=1, source_target_pairs={{16,0},{32,16},{48,32},{64,48},{80,64},{96,80},{112,96},{128,112},... | collective-permute-start | bytes 98312 | tf_op jit(solution)/shard_map/while/body/eval_jaxpr/ppermute | solution.py:25
  906.5 9.9 %collective-permute-start = (f32[8,1024]{1,0:T(8,128)S(1)}, f32[8,1024]{1,0:T(8,128)S(1)}, u32[]{:S(2)}, u32[]{:S(2)}) collective-permute-start(f32[8,1024]{1,0:T(8,128)S(1)} %all_gather.77), channel_id=1, source_target_pairs={{16,0},{32,16},{48,32},{64,48},{80,64},{96,80},{112,96},{128,112},... | collective-permute-start | bytes 98312 | tf_op jit(solution)/shard_map/while/body/eval_jaxpr/ppermute | solution.py:25
  934.9 9.9 %collective-permute-start = (f32[8,1024]{1,0:T(8,128)S(1)}, f32[8,1024]{1,0:T(8,128)S(1)}, u32[]{:S(2)}, u32[]{:S(2)}) collective-permute-start(f32[8,1024]{1,0:T(8,128)S(1)} %all_gather.77), channel_id=1, source_target_pairs={{16,0},{32,16},{48,32},{64,48},{80,64},{96,80},{112,96},{128,112},... | collective-permute-start | bytes 98312 | tf_op jit(solution)/shard_map/while/body/eval_jaxpr/ppermute | solution.py:25
  (24 other events, 1541.5 us)
Sparse Core Ops, SparseCore 0:
  17.0 41.1 all-gather.16
  87.3 53.4 all-gather.8
  161.3 54.2 all-gather.10
  217.3 36.5 all-gather.14
  255.5 56.7 all-gather.12
where the time goes:
time: 954 us; the launch traced here: 953 us
  blocking collectives  463 us (49%)
  waiting for transfers between devices  301 us (32%)
  starting transfers between devices  137 us (14%)
  matrix products  29.7 us (3%)
  between operations  13.6 us (1%)
    all_gather x15, blocking collectives, relay_back(): complete = lax.all_gather(emitted, 'blk', axis=1, tiled=True)  273 us
    ppermute x24, waiting for transfers between devices, shifted(): lax.ppermute(value, axis, [(source, source + steps) for source in range(i...  161 us
    ppermute x24, starting transfers between devices, shifted(): lax.ppermute(value, axis, [(source, source + steps) for source in range(i...  134 us
    all_gather x3, waiting for transfers between devices, on_device(): lax.all_gather(received_m, 'blk', axis=0, tiled=True)  98.7 us
    all_gather x4, blocking collectives, on_device(): lax.all_gather(received_v, 'blk', axis=1, tiled=True)  72.5 us
    all_gather x1, waiting for transfers between devices, on_device(): lax.all_gather(trans_mats[0], 'blk', axis=0, tiled=True)  41.3 us
    all_gather x1, blocking collectives, on_device(): lax.all_gather(inputs[0], 'blk', axis=1, tiled=True)  20.3 us
    all_gather x1, blocking collectives, on_device(): all_resid = lax.all_gather(residual, 'blk', axis=2, tiled=True)  19.8 us
  transfers between devices with their start and end apart: 31, of which 26 were waited for; matrix products, arithmetic and copies ran while one was open for 1% of the time, Pallas kernels for 0%

commit v1 on v0

--- a/solution.py
+++ b/solution.py
@@ -123,7 +123,11 @@
 
     def relay_back(relay_turn, later_now):
         emitted = apply_rows(backward_pair, later_now) + back_offset
-        complete = lax.all_gather(emitted, "blk", axis=1, tiled=True)
+        size = lax.axis_size("blk")
+        repeats = [size if d == 1 else 1 for d in range(emitted.ndim)]
+        complete = lax.all_to_all(
+            jnp.tile(emitted, repeats), "blk", split_axis=1, concat_axis=1, tiled=True
+        )
         received = shifted(complete, "tm", -1)
         return jnp.where(lax.axis_index("tm") == time_size - 2 - relay_turn, received, later_now)
 

time: 954 us -> 783 us (0.82)
  blocking collectives: 463 us -> 330 us
  waiting for transfers between devices: 301 us -> 266 us
    all_gather x15 -> x0, blocking collectives: 273 us -> none  [relay_back(): complete = lax.all_gather(emitted, 'blk', axis=1, tiled=True)]
    all_to_all x0 -> x15, blocking collectives: none -> 140 us  [relay_back(): lax.all_to_all(jnp.tile(emitted, repeats), 'blk', split_axis=1, concat_ax...]
    ppermute x24, waiting for transfers between devices: 161 us -> 126 us  [shifted(): lax.ppermute(value, axis, [(source, source + steps) for source in range(i...]
  transfers between devices with their start and end apart: 31 -> 31, of which waited for: 26 -> 26; matrix products, arithmetic and copies ran while one was open for 1% -> 2% of each run, Pallas kernels for 0% -> 0%
where the time goes in v1:
time: 783 us; the launch traced here: 781 us
  blocking collectives  330 us (42%)
  waiting for transfers between devices  266 us (34%)
  starting transfers between devices  132 us (17%)
  matrix products  29.7 us (4%)
  between operations  13.6 us (2%)
  local copies, waits for them, and re-layouts  7.9 us (1%)
    all_to_all x15, blocking collectives, relay_back(): lax.all_to_all(jnp.tile(emitted, repeats), 'blk', split_axis=1, concat_ax...  140 us
    ppermute x24, starting transfers between devices, shifted(): lax.ppermute(value, axis, [(source, source + steps) for source in range(i...  129 us
    ppermute x24, waiting for transfers between devices, shifted(): lax.ppermute(value, axis, [(source, source + steps) for source in range(i...  126 us
    all_gather x3, waiting for transfers between devices, on_device(): lax.all_gather(received_m, 'blk', axis=0, tiled=True)  98.7 us
    all_gather x4, blocking collectives, on_device(): lax.all_gather(received_v, 'blk', axis=1, tiled=True)  72.5 us
    all_gather x1, waiting for transfers between devices, on_device(): lax.all_gather(trans_mats[0], 'blk', axis=0, tiled=True)  41.3 us
    all_gather x1, blocking collectives, on_device(): lax.all_gather(inputs[0], 'blk', axis=1, tiled=True)  20.3 us
    all_gather x1, blocking collectives, on_device(): all_resid = lax.all_gather(residual, 'blk', axis=2, tiled=True)  19.8 us
  transfers between devices with their start and end apart: 31, of which 26 were waited for; matrix products, arithmetic and copies ran while one was open for 2% of the time, Pallas kernels for 0%

profile of v1, /device:TPU:7, one launch (start us, length us, event | category | flops | bytes accessed | tf_op | source)
XLA Modules:
  0.0 781.4 jit_solution(9297745965805951463)
XLA Ops:
  6.5 9.6 %all_gather.56 = bf16[2,128,1024]{2,1,0:T(8,128)(2,1)S(1)} all-gather(bf16[2,128,512]{2,1,0:T(8,128)(2,1)} %param.20), channel_id=1, replica_groups=mesh['tm'=16,'blk'=8,'samp'=2] {'samp'}, dimensions={2}, use_global_device_ids=true | all-gather | bytes 786432 | tf_op jit(solution)/shard_map/all_gather | solution.py:46
  16.9 41.3 %all-gather.17.cloned.1.call-done = bf16[1,1024,1024]{2,1,0:T(8,128)(2,1)} async-done(((bf16[1,128,1024]{2,1,0:T(8,128)(2,1)}), bf16[1,1024,1024]{2,1,0:T(8,128)(2,1)}) %all-gather.17.cloned.1.call-update) | async-done | bytes 2097168 | tf_op jit(solution)/shard_map/all_gather | solution.py:80
  87.2 53.6 %all-gather.9.cloned.1.call-done = f32[1024,1024]{1,0:T(8,128)} async-done(((f32[128,1024]{1,0:T(8,128)}), f32[1024,1024]{1,0:T(8,128)}) %all-gather.9.cloned.1.call-update) | async-done | bytes 4194320 | tf_op jit(solution)/shard_map/all_gather | solution.py:101
  148.7 11.6 %collective-permute-done.9 = f32[128,1024]{1,0:T(8,128)S(1)} collective-permute-done((f32[128,1024]{1,0:T(8,128)S(1)}, f32[128,1024]{1,0:T(8,128)S(1)}, u32[]{:S(2)}, u32[]{:S(2)}) %collective-permute-start.9) | collective-permute-done | bytes 524320 | tf_op jit(solution)/shard_map/ppermute | solution.py:25
  170.5 45.1 %all-gather.11.cloned.1.call-done = f32[1024,1024]{1,0:T(8,128)} async-done(((f32[128,1024]{1,0:T(8,128)}), f32[1024,1024]{1,0:T(8,128)}) %all-gather.11.cloned.1.call-update) | async-done | bytes 4194320 | tf_op jit(solution)/shard_map/all_gather | solution.py:101
  224.2 12.2 %collective-permute-done.11 = f32[128,1024]{1,0:T(8,128)S(1)} collective-permute-done((f32[128,1024]{1,0:T(8,128)S(1)}, f32[128,1024]{1,0:T(8,128)S(1)}, u32[]{:S(2)}, u32[]{:S(2)}) %collective-permute-start.11) | collective-permute-done | bytes 524320 | tf_op jit(solution)/shard_map/ppermute | solution.py:25
  246.9 19.8 %all_gather.53 = f32[2,8,256]{1,0,2:T(2,128)S(1)} all-gather(f32[2,8,32]{1,0,2:T(2,128)S(1)} %copy.27), channel_id=1, replica_groups=mesh['tm'=16,'blk'=8,'samp'=2] {'blk'}, dimensions={2}, use_global_device_ids=true | all-gather | bytes 18432 | tf_op jit(solution)/shard_map/all_gather | solution.py:74
  267.0 20.3 %all-gather.1 = f32[1,8,1024]{2,1,0:T(8,128)S(1)} all-gather(f32[1,8,128]{2,1,0:T(8,128)S(1)} %slice.52), channel_id=3, replica_groups=mesh['tm'=16,'blk'=8,'samp'=2] {'blk'}, dimensions={2}, use_global_device_ids=true | all-gather | bytes 36864 | tf_op jit(solution)/shard_map/all_gather | solution.py:89
  287.5 16.8 %collective-permute-start.3 = (f32[8,128]{1,0:T(8,128)S(1)}, f32[8,128]{1,0:T(8,128)S(1)}, u32[]{:S(2)}, u32[]{:S(2)}) collective-permute-start(f32[8,128]{1,0:T(8,128)S(1)} %convolution_add_fusion.4), channel_id=1, source_target_pairs={{0,16},{16,32},{32,48},{48,64},{64,80},{80,96},{96,112},{112,128},... | collective-permute-start | bytes 12296 | tf_op jit(solution)/shard_map/ppermute | solution.py:25
  312.1 18.1 %all_gather.57 = f32[8,1024]{1,0:T(8,128)S(1)} all-gather(f32[8,128]{1,0:T(8,128)S(1)} %collective-permute-done.4), channel_id=1, replica_groups=mesh['tm'=16,'blk'=8,'samp'=2] {'blk'}, dimensions={1}, use_global_device_ids=true | all-gather | bytes 36864 | tf_op jit(solution)/shard_map/all_gather | solution.py:102
  335.1 18.1 %all_gather.59 = f32[8,1024]{1,0:T(8,128)S(1)} all-gather(f32[8,128]{1,0:T(8,128)S(1)} %collective-permute-done.6), channel_id=1, replica_groups=mesh['tm'=16,'blk'=8,'samp'=2] {'blk'}, dimensions={1}, use_global_device_ids=true | all-gather | bytes 36864 | tf_op jit(solution)/shard_map/all_gather | solution.py:102
  359.5 18.3 %all_gather.61 = f32[8,1024]{1,0:T(8,128)S(1)} all-gather(f32[8,128]{1,0:T(8,128)S(1)} %collective-permute-done.8), channel_id=1, replica_groups=mesh['tm'=16,'blk'=8,'samp'=2] {'blk'}, dimensions={1}, use_global_device_ids=true | all-gather | bytes 36864 | tf_op jit(solution)/shard_map/all_gather | solution.py:102
  381.8 18.1 %all_gather.63 = f32[8,1024]{1,0:T(8,128)S(1)} all-gather(f32[8,128]{1,0:T(8,128)S(1)} %collective-permute-done.10), channel_id=1, replica_groups=mesh['tm'=16,'blk'=8,'samp'=2] {'blk'}, dimensions={1}, use_global_device_ids=true | all-gather | bytes 36864 | tf_op jit(solution)/shard_map/all_gather | solution.py:102
  405.0 18.2 %all_gather.65 = f32[8,1024]{1,0:T(8,128)S(1)} all-gather(f32[8,128]{1,0:T(8,128)S(1)} %convolution_add_fusion.7), channel_id=1, replica_groups=mesh['tm'=16,'blk'=8,'samp'=2] {'blk'}, dimensions={1}, use_global_device_ids=true | all-gather | bytes 36864 | tf_op jit(solution)/shard_map/all_gather | solution.py:108
  424.2 18.2 %all_gather.66 = f32[2,8,1024]{2,1,0:T(8,128)S(1)} all-gather(f32[2,8,128]{2,1,0:T(8,128)S(1)} %fusion.18), channel_id=1, replica_groups=mesh['tm'=16,'blk'=8,'samp'=2] {'blk'}, dimensions={2}, use_global_device_ids=true | all-gather | bytes 73728 | tf_op jit(solution)/shard_map/all_gather | solution.py:117
  442.9 18.1 %all_gather.67 = f32[8,1024]{1,0:T(8,128)S(1)} all-gather(f32[8,128]{1,0:T(8,128)S(1)} %fusion.19), channel_id=1, replica_groups=mesh['tm'=16,'blk'=8,'samp'=2] {'blk'}, dimensions={1}, use_global_device_ids=true | all-gather | bytes 36864 | tf_op jit(solution)/shard_map/all_gather | solution.py:121
  461.3 312.2 %while.14 = (s32[]{:T(128)}, f32[8,1024]{1,0:T(8,128)S(1)}, f32[128,1024]{1,0:T(8,128)S(1)}, f32[8,128]{1,0:T(8,128)S(1)}, s32[]{:T(128)}, /*index=5*/s32[]{:T(128)}, u32[]{:T(128)}, u32[]{:T(128)}, s32[]{:T(128)}) while((s32[]{:T(128)}, f32[8,1024]{1,0:T(8,128)S(1)}, f32[128,1024]{1,0:T(8,128)S(1)}, f32[8,128]{1,0:T(8,128)S(1)}, ...), condition=%wide.region_2.3_spmd.clone, body=%wide.region_1.2_spmd.clone.sunk | while | flops 12608520 | bytes 897222 | solution.py:134
  461.9 10.5 %all_to_all.15 = f32[8,8,128]{2,0,1:T(8,128)S(1)} all-to-all(f32[8,8,128]{2,0,1:T(8,128)S(1)} %tile.19), channel_id=1, replica_groups=mesh['tm'=16,'blk'=8,'samp'=2] {'blk'}, dimensions={1} | all-to-all | bytes 65536 | tf_op jit(solution)/shard_map/while/body/eval_jaxpr/all_to_all | solution.py:128
  472.4 52.7 %collective-permute-start = (f32[8,1024]{1,0:T(8,128)S(1)}, f32[8,1024]{1,0:T(8,128)S(1)}, u32[]{:S(2)}, u32[]{:S(2)}) collective-permute-start(f32[8,1024]{1,0:T(8,128)S(1)} %bitcast.98), channel_id=1, source_target_pairs={{16,0},{32,16},{48,32},{64,48},{80,64},{96,80},{112,96},{128,112},... | collective-permute-start | bytes 98312 | tf_op jit(solution)/shard_map/while/body/eval_jaxpr/ppermute | solution.py:25
  534.3 9.2 %all_to_all.15 = f32[8,8,128]{2,0,1:T(8,128)S(1)} all-to-all(f32[8,8,128]{2,0,1:T(8,128)S(1)} %tile.19), channel_id=1, replica_groups=mesh['tm'=16,'blk'=8,'samp'=2] {'blk'}, dimensions={1} | all-to-all | bytes 65536 | tf_op jit(solution)/shard_map/while/body/eval_jaxpr/all_to_all | solution.py:128
  551.4 9.2 %all_to_all.15 = f32[8,8,128]{2,0,1:T(8,128)S(1)} all-to-all(f32[8,8,128]{2,0,1:T(8,128)S(1)} %tile.19), channel_id=1, replica_groups=mesh['tm'=16,'blk'=8,'samp'=2] {'blk'}, dimensions={1} | all-to-all | bytes 65536 | tf_op jit(solution)/shard_map/while/body/eval_jaxpr/all_to_all | solution.py:128
  568.6 9.2 %all_to_all.15 = f32[8,8,128]{2,0,1:T(8,128)S(1)} all-to-all(f32[8,8,128]{2,0,1:T(8,128)S(1)} %tile.19), channel_id=1, replica_groups=mesh['tm'=16,'blk'=8,'samp'=2] {'blk'}, dimensions={1} | all-to-all | bytes 65536 | tf_op jit(solution)/shard_map/while/body/eval_jaxpr/all_to_all | solution.py:128
  619.9 9.2 %all_to_all.15 = f32[8,8,128]{2,0,1:T(8,128)S(1)} all-to-all(f32[8,8,128]{2,0,1:T(8,128)S(1)} %tile.19), channel_id=1, replica_groups=mesh['tm'=16,'blk'=8,'samp'=2] {'blk'}, dimensions={1} | all-to-all | bytes 65536 | tf_op jit(solution)/shard_map/while/body/eval_jaxpr/all_to_all | solution.py:128
  688.4 9.2 %all_to_all.15 = f32[8,8,128]{2,0,1:T(8,128)S(1)} all-to-all(f32[8,8,128]{2,0,1:T(8,128)S(1)} %tile.19), channel_id=1, replica_groups=mesh['tm'=16,'blk'=8,'samp'=2] {'blk'}, dimensions={1} | all-to-all | bytes 65536 | tf_op jit(solution)/shard_map/while/body/eval_jaxpr/all_to_all | solution.py:128
  (194 shorter events, 300.8 us)
Async XLA Ops:
  6.5 51.7 %all-gather.17.cloned.1.call-start = ((), (), s32[]{:S(2)}) async-start(), calls=%async_computation.5 | async-start | bytes 2359296 | tf_op jit(solution)/shard_map/all_gather | solution.py:80
  16.9 123.9 %all-gather.9.cloned.1.call-start = ((), (), s32[]{:S(2)}) async-start(), calls=%async_computation.1 | async-start | bytes 4718592 | tf_op jit(solution)/shard_map/all_gather | solution.py:101
  60.3 13.5 %collective-permute-start.5 = (f32[128,1024]{1,0:T(8,128)S(1)}, f32[128,1024]{1,0:T(8,128)S(1)}, u32[]{:S(2)}, u32[]{:S(2)}) collective-permute-start(f32[128,1024]{1,0:T(8,128)S(1)} %fusion.4), channel_id=1, source_target_pairs={{0,16},{16,32},{32,48},{48,64},{64,80},{80,96},{96,112},{112,128},... | collective-permute-start | bytes 1572872 | tf_op jit(solution)/shard_map/ppermute | solution.py:25
  73.7 12.6 %collective-permute-start.7 = (f32[128,1024]{1,0:T(8,128)S(1)}, f32[128,1024]{1,0:T(8,128)S(1)}, u32[]{:S(2)}, u32[]{:S(2)}) collective-permute-start(f32[128,1024]{1,0:T(8,128)S(1)} %collective-permute-done.5), channel_id=1, source_target_pairs={{0,16},{16,32},{32,48},{48,64},{64,80},{80,96},{96,112},{112,128},... | collective-permute-start | bytes 1572872 | tf_op jit(solution)/shard_map/ppermute | solution.py:25
  87.2 128.5 %all-gather.11.cloned.1.call-start = ((), (), s32[]{:S(2)}) async-start(), calls=%async_computation.2 | async-start | bytes 4718592 | tf_op jit(solution)/shard_map/all_gather | solution.py:101
  145.5 14.8 %collective-permute-start.9 = (f32[128,1024]{1,0:T(8,128)S(1)}, f32[128,1024]{1,0:T(8,128)S(1)}, u32[]{:S(2)}, u32[]{:S(2)}) collective-permute-start(f32[128,1024]{1,0:T(8,128)S(1)} %fusion.29), channel_id=1, source_target_pairs={{0,32},{16,48},{32,64},{48,80},{64,96},{80,112},{96,128},{112,144}... | collective-permute-start | bytes 1572872 | tf_op jit(solution)/shard_map/ppermute | solution.py:25
  161.2 218.6 %all-gather.15.cloned.1.call-start = ((), (), s32[]{:S(2)}) async-start(), calls=%async_computation.4 | async-start | bytes 2359296 | tf_op jit(solution)/shard_map/all_gather | solution.py:85
  170.5 229.5 %all-gather.13.cloned.1.call-start = ((), (), s32[]{:S(2)}) async-start(), calls=%async_computation.3 | async-start | bytes 4718592 | tf_op jit(solution)/shard_map/all_gather | solution.py:101
  220.2 16.2 %collective-permute-start.11 = (f32[128,1024]{1,0:T(8,128)S(1)}, f32[128,1024]{1,0:T(8,128)S(1)}, u32[]{:S(2)}, u32[]{:S(2)}) collective-permute-start(f32[128,1024]{1,0:T(8,128)S(1)} %fusion.30), channel_id=1, source_target_pairs={{0,64},{16,80},{32,96},{48,112},{64,128},{80,144},{96,160},{112,17... | collective-permute-start | bytes 1572872 | tf_op jit(solution)/shard_map/ppermute | solution.py:25
  237.4 8.5 %collective-permute-start.1 = (f32[2,8,16]{2,1,0:T(8,128)S(1)}, f32[2,8,16]{2,1,0:T(8,128)S(1)}, u32[]{:S(2)}, u32[]{:S(2)}) collective-permute-start(f32[2,8,16]{2,1,0:T(8,128)S(1)} %get-tuple-element.108), channel_id=1, source_target_pairs={{0,2},{2,4},{4,6},{6,8},{8,10},{10,12},{12,14},{14,0},{1,3},{3,5},... | collective-permute-start | bytes 3080 | tf_op jit(solution)/shard_map/ppermute | solution.py:16
  237.4 8.5 %collective-permute-start.2 = (f32[2,8,16]{2,1,0:T(8,128)S(1)}, f32[2,8,16]{2,1,0:T(8,128)S(1)}, u32[]{:S(2)}, u32[]{:S(2)}) collective-permute-start(f32[2,8,16]{2,1,0:T(8,128)S(1)} %get-tuple-element.109), channel_id=1, source_target_pairs={{2,0},{4,2},{6,4},{8,6},{10,8},{12,10},{14,12},{0,14},{3,1},{5,3},... | collective-permute-start | bytes 3080 | tf_op jit(solution)/shard_map/ppermute | solution.py:17
  287.5 17.6 %collective-permute-start.3 = (f32[8,128]{1,0:T(8,128)S(1)}, f32[8,128]{1,0:T(8,128)S(1)}, u32[]{:S(2)}, u32[]{:S(2)}) collective-permute-start(f32[8,128]{1,0:T(8,128)S(1)} %convolution_add_fusion.4), channel_id=1, source_target_pairs={{0,16},{16,32},{32,48},{48,64},{64,80},{80,96},{96,112},{112,128},... | collective-permute-start | bytes 12296 | tf_op jit(solution)/shard_map/ppermute | solution.py:25
  472.4 61.4 %collective-permute-start = (f32[8,1024]{1,0:T(8,128)S(1)}, f32[8,1024]{1,0:T(8,128)S(1)}, u32[]{:S(2)}, u32[]{:S(2)}) collective-permute-start(f32[8,1024]{1,0:T(8,128)S(1)} %bitcast.98), channel_id=1, source_target_pairs={{16,0},{32,16},{48,32},{64,48},{80,64},{96,80},{112,96},{128,112},... | collective-permute-start | bytes 98312 | tf_op jit(solution)/shard_map/while/body/eval_jaxpr/ppermute | solution.py:25
  543.6 7.3 collective-permute-start
  560.7 7.3 collective-permute-start
  577.8 7.3 collective-permute-start
  594.9 7.3 collective-permute-start
  612.0 7.3 collective-permute-start
  629.2 7.3 collective-permute-start
  646.3 7.3 collective-permute-start
  663.4 7.3 collective-permute-start
  680.5 7.3 collective-permute-start
  697.6 7.3 collective-permute-start
  714.8 7.3 collective-permute-start
  (24 other events, 1536.6 us)
Sparse Core Ops, SparseCore 0:
  17.0 41.1 all-gather.16
  87.3 53.4 all-gather.8
  161.3 54.2 all-gather.10
  217.3 36.5 all-gather.14
  255.5 56.7 all-gather.12
